TPU v7x, 128 devices: a whole 4x4x4 slice. The times are simulated.
128 devices in a mesh: ctx: 4 (over z_lo, core), tp: 16 (over y, x), dp: 2 (over z_hi).
Axes of the slice: x: 4, y: 4, z: 4 (z_hi: 2, z_lo: 2; z = z_hi * 2 + z_lo), core: 2. Of those that a mesh axis runs over, the one named last changes fastest.
Arguments:
- hidden_in: bfloat16 [8192, 8192], P(('dp', 'ctx', 'tp')), parts along dimension 0
- norm_gain: float32 [8192], replicated
- q_weight: bfloat16 [8192, 8192], P(None, 'tp')
- kv_weight: bfloat16 [8192, 2048], P(None, 'tp')
- out_weight: bfloat16 [8192, 8192], P('tp'), may hold values from -0.25 to 0.25
- doc_lengths: int32 [16], P('dp'), parts along dimension 0, may hold values from 1 to 2048, 4096 in all
Outputs:
- attn_out: bfloat16 [8192, 8192], P(('dp', 'ctx', 'tp')), parts along dimension 0
There are 2 independent parts, one for each index of `dp`. A program takes and returns all parts, laid end to end along the dimension named above; an argument that names none is the same for every part. Nothing has to cross between parts.
Inputs may be any that keep to these rules, and one draw needn't show every extreme that they name: `doc_lengths`: the lengths of a row sum to 4096; the longest document has exactly 2048 tokens.
All inputs are finite; a program needn't handle non-finite values.
Results may differ from a plain program's by a relative error of at most 0.015.
The roundings to bfloat16 on the way count: a program that leaves them out, or rounds other values in their place, can miss the bound.
Values may be sent and summed in bfloat16 or wider, within the bound.
No kernel may reach another device: no remote copies, remote signals or barrier semaphores. Data moves between devices by JAX's collectives and lax.ppermute only.
A program may use at most 128 MiB of HBM per device.

v0:
```python
import math
import jax
import jax.numpy as jnp
from jax import lax
from jax.sharding import PartitionSpec as P

QH = 64
KVH = 8
HD = 128


def from_everyone(shard, axis):
    length = lax.axis_size(axis)
    return lax.all_to_all(
        jnp.broadcast_to(shard[None], (length, *shard.shape)), axis, 0, 0, tiled=True
    )


def laid_out(blocks, dim):
    blocks = jnp.moveaxis(blocks, 0, dim)
    shape = blocks.shape
    return blocks.reshape(*shape[:dim], shape[dim] * shape[dim + 1], *shape[dim + 2 :])


def gathered_copies(shard, axis, dim):
    blocks = from_everyone(shard, axis)
    return laid_out(blocks, dim)


def doc_index(positions, ends):
    return jnp.sum((positions[:, None] >= ends[None, :]).astype(jnp.int32), axis=1)


def doc_start(positions, lengths, ends):
    return jnp.sum(jnp.where(positions[:, None] >= ends[None, :], lengths[None, :], 0), axis=1)


def rope_freqs(half):
    base = jnp.power(jnp.float32(500000.0), -(jnp.arange(half, dtype=jnp.float32) * 2.0) / HD)
    wavelen = 2.0 * math.pi / base
    smooth = (8192.0 / wavelen - 1.0) / 3.0
    middle = (1.0 - smooth) * base / 8.0 + smooth * base
    return jnp.where(wavelen < 2048.0, base, jnp.where(wavelen > 8192.0, base / 8.0, middle))


def rotate(values, within):
    rows = values.shape[0]
    blocks = values.reshape(rows, values.shape[1] // HD, HD)
    half = HD // 2
    freqs = rope_freqs(half)
    angles = within.astype(jnp.float32)[:, None] * freqs[None, :]
    cosine = jnp.cos(angles)[:, None, :]
    sine = jnp.sin(angles)[:, None, :]
    first = blocks[:, :, :half]
    second = blocks[:, :, half:]
    turned = jnp.concatenate(
        [first * cosine - second * sine, second * cosine + first * sine], axis=2
    )
    return turned.reshape(rows, values.shape[1])


def local(hidden_in, norm_gain, q_weight, kv_weight, out_weight, doc_lengths):
    tok_rows = hidden_in.shape[0]
    n_tp = lax.axis_size("tp")
    n_ctx = lax.axis_size("ctx")
    ctx_rows = tok_rows * n_tp
    block_rows = ctx_rows // n_ctx
    q_cols = q_weight.shape[1]
    heads_here = q_cols // HD
    group = QH // KVH
    kv_here = max(1, heads_here // group)
    sub_heads = heads_here // kv_here
    kv_cols = kv_weight.shape[1]
    tp_index = lax.axis_index("tp")
    ctx_index = lax.axis_index("ctx")
    scale = HD ** (-0.5)
    x = hidden_in.astype(jnp.float32)
    normed = (
        x * lax.rsqrt(jnp.mean(x * x, axis=1, keepdims=True) + 1e-05) * norm_gain[None, :]
    ).astype(jnp.bfloat16)
    ends = jnp.cumsum(doc_lengths)
    is_key = tp_index * kv_cols < KVH * HD
    piece = lax.all_gather(normed, "tp", axis=0, tiled=True)
    count = piece.shape[0]
    positions = ctx_index * ctx_rows + jnp.arange(count, dtype=jnp.int32)
    within = positions - doc_start(positions, doc_lengths, ends)
    q_raw = jnp.dot(piece, q_weight, preferred_element_type=jnp.float32)
    kv_raw = jnp.dot(piece, kv_weight, preferred_element_type=jnp.float32)
    q_done = rotate(q_raw, within).astype(jnp.bfloat16)
    kv_done = jnp.where(is_key, rotate(kv_raw, within), kv_raw).astype(jnp.bfloat16)
    projected = jnp.concatenate([q_done, kv_done], axis=1)
    queries = projected[:, :q_cols]
    kv_part = projected[:, q_cols:]
    kv_every = lax.all_gather(kv_part, "tp", axis=1, tiled=True)
    first_kv = tp_index * heads_here // group
    key_cols = lax.dynamic_slice_in_dim(kv_every, first_kv * HD, kv_here * HD, 1)
    value_cols = lax.dynamic_slice_in_dim(kv_every, KVH * HD + first_kv * HD, kv_here * HD, 1)
    kv_mine = jnp.concatenate([key_cols, value_cols], axis=1)
    block_starts = [ctx_index * ctx_rows + b * block_rows for b in range(n_ctx)]
    q_blocks = queries.reshape(n_ctx, block_rows, kv_here, sub_heads, HD).transpose(0, 2, 3, 1, 4)
    q_positions = [
        start_row + jnp.arange(block_rows, dtype=jnp.int32) for start_row in block_starts
    ]
    q_docs = [doc_index(pos, ends) for pos in q_positions]
    piece = gathered_copies(kv_mine, "ctx", 0)
    top_all = jnp.full((n_ctx, kv_here, sub_heads, block_rows), -1e30, jnp.float32)
    total_all = jnp.zeros((n_ctx, kv_here, sub_heads, block_rows), jnp.float32)
    acc_all = jnp.zeros((n_ctx, kv_here, sub_heads, block_rows, HD), jnp.float32)
    count = piece.shape[0]
    key_piece = piece[:, : kv_here * HD].reshape(count, kv_here, HD)
    value_piece = piece[:, kv_here * HD :].reshape(count, kv_here, HD)
    key_pos = jnp.arange(count, dtype=jnp.int32)
    key_doc = doc_index(key_pos, ends)
    new_top = []
    new_total = []
    new_acc = []
    for block in range(n_ctx):
        q_here = q_blocks[block]
        q_pos = q_positions[block]
        q_doc = q_docs[block]
        state = (top_all[block], total_all[block], acc_all[block])
        top_old, total_old, acc_old = state
        scores = (
            jnp.einsum("ghqd,kgd->ghqk", q_here, key_piece, preferred_element_type=jnp.float32)
            * scale
        )
        visible = (key_doc[None, :] == q_doc[:, None]) & (key_pos[None, :] <= q_pos[:, None])
        scores = jnp.where(visible[None, None], scores, jnp.float32(-1e30))
        top_new = jnp.maximum(top_old, jnp.max(scores, axis=3))
        expd = jnp.where(
            visible[None, None], jnp.exp(scores - top_new[..., None]), jnp.float32(0.0)
        )
        total_new = jnp.sum(expd, axis=3)
        acc_new = jnp.einsum(
            "ghqk,kgd->ghqd",
            expd.astype(jnp.bfloat16),
            value_piece,
            preferred_element_type=jnp.float32,
        )
        state = (top_new, total_new, acc_new)
        new_top.append(state[0])
        new_total.append(state[1])
        new_acc.append(state[2])
    total_all = jnp.stack(new_total)
    acc_all = jnp.stack(new_acc)
    heads_out = (acc_all / total_all[..., None]).astype(jnp.bfloat16)
    heads_out = heads_out.transpose(0, 3, 1, 2, 4).reshape(ctx_rows, q_cols)
    return lax.psum_scatter(
        jnp.dot(heads_out, out_weight, preferred_element_type=jnp.float32).astype(jnp.bfloat16),
        "tp",
        scatter_dimension=0,
        tiled=True,
    )


def solution(mesh):
    placed = (
        P(("dp", "ctx", "tp"), None),
        P(),
        P(None, "tp"),
        P(None, "tp"),
        P("tp", None),
        P("dp"),
    )
    return jax.shard_map(
        local, mesh=mesh, in_specs=placed, out_specs=P(("dp", "ctx", "tp"), None), check_vma=False
    )
```

profile of v0, /device:TPU:1, one launch (start us, length us, event | category | flops | bytes accessed | tf_op | source)
XLA Modules:
  0.0 425.1 jit_solution(6359207053137103046)
XLA Ops:
  6.5 1.7 fusion.28
  8.2 2.5 fusion.30
  10.7 0.0 all-gather.3.cloned.1.call-update
  10.8 0.0 all-gather.5.cloned.1.call-start
  10.8 0.8 reduce-window.8
  11.7 0.7 select_reduce_fusion
  12.5 112.6 %all-gather.3.cloned.1.call-done = bf16[1024,8192]{1,0:T(8,128)(2,1)} async-done(((bf16[64,8192]{1,0:T(8,128)(2,1)}), bf16[1024,8192]{1,0:T(8,128)(2,1)}) %all-gather.3.cloned.1.call-update) | async-done | bytes 16777232 | tf_op jit(solution)/shard_map/all_gather | solution.py:83
  125.0 11.4 %fusion.73 = f32[1024,128]{0,1:T(8,128)S(1)} fusion(bf16[1024,8192]{1,0:T(8,128)(2,1)} %all-gather.3.cloned.1.call-done, bf16[8192,128]{1,0:T(8,128)(2,1)S(1)} %copy-done), kind=kOutput, calls=%fused_computation.116 | convolution fusion | flops 2147483648 | bytes 19398656 | tf_op jit(solution)/shard_map/dot_general | solution.py:88
  136.5 1.2 fusion.57
  137.6 0.8 fusion.48
  138.4 0.0 all-gather.5.cloned.1.call-update
  138.5 0.1 convert_reduce_fusion.4
  138.6 0.1 convert_reduce_fusion
  138.7 3.1 multiply_cosine_fusion
  141.7 6.3 %fusion.24 = (pred[256,4096]{1,0:T(8,128)(4,1)}, pred[256,4096]{1,0:T(8,128)(4,1)}, pred[256,4096]{1,0:T(8,128)(4,1)}, pred[256,4096]{1,0:T(8,128)(4,1)S(1)}) fusion(s32[256]{0:T(256)S(1)} %iota_add_fusion.4, s32[4096]{0:T(1024)S(1)} %convert_reduce_fusion, s32[256]{0:T(256)S(1)} %get-tuple-element.5, s32[256]{0:T(256)S(1)} %iota_add_fusion.3, ...), kind=kLoop, calls=%fused_computation.33 | loop fusion | flops 12582912 | bytes 4218880 | tf_op jit(solution)/shard_map/and | solution.py:127
  148.1 41.5 %all-gather.5.cloned.1.call-done = bf16[1024,2048]{0,1:T(8,128)(2,1)} async-done(((bf16[1024,128]{0,1:T(8,128)(2,1)}), bf16[1024,2048]{0,1:T(8,128)(2,1)}) %all-gather.5.cloned.1.call-update) | async-done | bytes 4194320 | tf_op jit(solution)/shard_map/all_gather | solution.py:94
  189.6 1.1 constant_dynamic-slice_fusion.1
  190.7 0.2 copy.16
  190.9 1.4 broadcast_in_dim.65
  192.3 5.2 %all-to-all-start = ((bf16[4,1024,256]{2,1,0:T(8,128)(2,1)}), bf16[4,1024,256]{2,1,0:T(8,128)(2,1)}, u32[]{:S(2)}, u32[]{:S(2)}) async-start(bf16[4,1024,256]{2,1,0:T(8,128)(2,1)} %broadcast_in_dim.65), calls=%async_computation | async-start | bytes 4194304 | tf_op jit(solution)/shard_map/all_to_all | solution.py:14
  197.5 0.5 reduce-scatter.2.cloned.1.call-start
  198.1 17.2 %fusion.72 = f32[1024,512]{0,1:T(8,128)S(1)} fusion(bf16[1024,8192]{1,0:T(8,128)(2,1)} %all-gather.3.cloned.1.call-done, bf16[8192,512]{1,0:T(8,128)(2,1)} %param.8), kind=kOutput, calls=%fused_computation.115 | convolution fusion | flops 8589934592 | bytes 27262976 | tf_op jit(solution)/shard_map/dot_general | solution.py:87
  215.3 1.6 fusion.71
  216.9 1.8 copy.19
  218.7 3.2 copy.18
  221.9 2.4 subtract_convert_fusion
  224.3 0.0 copy-start.4
  224.3 0.6 pad_maximum_fusion
  224.9 1.1 copy.26
  226.0 0.0 all-to-all-done
  226.0 5.0 %fusion = (f32[4,256]{1,0:T(4,128)S(1)}, f32[4,256,4096]{2,1,0:T(8,128)S(1)}) fusion(pred[256,4096]{1,0:T(8,128)(4,1)} %get-tuple-element.17, bf16[4096,256]{1,0:T(8,128)(2,1)} %bitcast.8, bf16[4,1,4,256,128]{4,3,2,1,0:T(8,128)(2,1)} %bitcast.85), kind=kOutput, calls=%fused_computation.9 | convolution fusion | flops 1086323712 | bytes 19140608 | tf_op jit(solution)/shard_map/ghqd,kgd->ghqk/dot_general | solution.py:124
  231.0 5.2 %fusion.4 = f32[4,256]{1,0:T(4,128)S(1)} fusion(f32[4,256,4096]{2,1,0:T(8,128)S(1)} %get-tuple-element.30, f32[4,256]{1,0:T(4,128)S(1)} %broadcast_maximum_fusion.3, pred[256,4096]{1,0:T(8,128)(4,1)S(1)} %copy-done.4), kind=kLoop, calls=%fused_computation.13 | loop fusion | flops 20970496 | bytes 17833984 | tf_op jit(solution)/shard_map/reduce_sum | solution.py:133
  236.3 6.3 %fusion.32 = f32[1,1,4,256,128]{4,3,2,1,0:T(8,128)S(1)} fusion(f32[4,256,4096]{2,1,0:T(8,128)S(1)} %get-tuple-element.30, f32[4,256]{1,0:T(4,128)S(1)} %broadcast_maximum_fusion.3, pred[256,4096]{1,0:T(8,128)(4,1)S(1)} %copy-done.5, bf16[4096,256]{1,0:T(8,128)(2,1)} %bitcast.8), kind=kOutput, calls=%fused_computation.46 | convolution fusion | flops 1094713344 | bytes 19402752 | tf_op jit(solution)/shard_map/ghqk,kgd->ghqd/dot_general | solution.py:134
  242.6 4.7 %fusion.1 = (f32[4,256]{1,0:T(4,128)S(1)}, f32[4,256,4096]{2,1,0:T(8,128)S(1)}) fusion(pred[256,4096]{1,0:T(8,128)(4,1)S(1)} %copy-done.3, bf16[4096,256]{1,0:T(8,128)(2,1)} %bitcast.8, bf16[4,1,4,256,128]{4,3,2,1,0:T(8,128)(2,1)S(1)} %bitcast.86), kind=kOutput, calls=%fused_computation.10 | convolution fusion | flops 1086323712 | bytes 19140608 | tf_op jit(solution)/shard_map/ghqd,kgd->ghqk/dot_general | solution.py:124
  247.3 5.3 %fusion.6 = f32[4,256]{1,0:T(4,128)S(1)} fusion(f32[4,256,4096]{2,1,0:T(8,128)S(1)} %get-tuple-element.28, f32[4,256]{1,0:T(4,128)S(1)} %broadcast_maximum_fusion.2, pred[256,4096]{1,0:T(8,128)(4,1)S(1)} %copy-done.3), kind=kLoop, calls=%fused_computation.15 | loop fusion | flops 20970496 | bytes 17833984 | tf_op jit(solution)/shard_map/reduce_sum | solution.py:133
  252.6 6.2 %fusion.35 = f32[1,1,4,256,128]{4,3,2,1,0:T(8,128)S(1)} fusion(f32[4,256,4096]{2,1,0:T(8,128)S(1)} %get-tuple-element.28, f32[4,256]{1,0:T(4,128)S(1)} %broadcast_maximum_fusion.2, pred[256,4096]{1,0:T(8,128)(4,1)S(1)} %copy-done.3, bf16[4096,256]{1,0:T(8,128)(2,1)} %bitcast.8), kind=kOutput, calls=%fused_computation.47 | convolution fusion | flops 1094713344 | bytes 19402752 | tf_op jit(solution)/shard_map/ghqk,kgd->ghqd/dot_general | solution.py:134
  258.8 4.7 %fusion.2 = (f32[4,256]{1,0:T(4,128)S(1)}, f32[4,256,4096]{2,1,0:T(8,128)S(1)}) fusion(pred[256,4096]{1,0:T(8,128)(4,1)S(1)} %copy-done.2, bf16[4096,256]{1,0:T(8,128)(2,1)} %bitcast.8, bf16[4,1,4,256,128]{4,3,2,1,0:T(8,128)(2,1)S(1)} %bitcast.87), kind=kOutput, calls=%fused_computation.11 | convolution fusion | flops 1086323712 | bytes 19140608 | tf_op jit(solution)/shard_map/ghqd,kgd->ghqk/dot_general | solution.py:124
  263.6 5.3 %fusion.8 = f32[4,256]{1,0:T(4,128)S(1)} fusion(f32[4,256,4096]{2,1,0:T(8,128)S(1)} %get-tuple-element.26, f32[4,256]{1,0:T(4,128)S(1)} %broadcast_maximum_fusion.1, pred[256,4096]{1,0:T(8,128)(4,1)S(1)} %copy-done.2), kind=kLoop, calls=%fused_computation.17 | loop fusion | flops 20970496 | bytes 17833984 | tf_op jit(solution)/shard_map/reduce_sum | solution.py:133
  268.9 6.1 %fusion.38 = f32[1,1,4,256,128]{4,3,2,1,0:T(8,128)S(1)} fusion(f32[4,256,4096]{2,1,0:T(8,128)S(1)} %get-tuple-element.26, f32[4,256]{1,0:T(4,128)S(1)} %broadcast_maximum_fusion.1, pred[256,4096]{1,0:T(8,128)(4,1)S(1)} %copy-done.2, bf16[4096,256]{1,0:T(8,128)(2,1)} %bitcast.8), kind=kOutput, calls=%fused_computation.48 | convolution fusion | flops 1094713344 | bytes 19402752 | tf_op jit(solution)/shard_map/ghqk,kgd->ghqd/dot_general | solution.py:134
  275.0 4.7 %fusion.3 = (f32[4,256]{1,0:T(4,128)S(1)}, f32[4,256,4096]{2,1,0:T(8,128)S(1)}) fusion(pred[256,4096]{1,0:T(8,128)(4,1)S(1)} %get-tuple-element.20, bf16[4096,256]{1,0:T(8,128)(2,1)} %bitcast.8, bf16[4,1,4,256,128]{4,3,2,1,0:T(8,128)(2,1)S(1)} %bitcast.88), kind=kOutput, calls=%fused_computation.12 | convolution fusion | flops 1086323712 | bytes 19140608 | tf_op jit(solution)/shard_map/ghqd,kgd->ghqk/dot_general | solution.py:124
  279.7 6.1 %fusion.41 = f32[1,1,4,256,128]{4,3,2,1,0:T(8,128)S(1)} fusion(f32[4,256,4096]{2,1,0:T(8,128)S(1)} %get-tuple-element.24, f32[4,256]{1,0:T(4,128)S(1)} %broadcast_maximum_fusion, pred[256,4096]{1,0:T(8,128)(4,1)S(1)} %get-tuple-element.20, bf16[4096,256]{1,0:T(8,128)(2,1)} %bitcast.8), kind=kOutput, calls=%fused_computation.49 | convolution fusion | flops 1094713344 | bytes 19402752 | tf_op jit(solution)/shard_map/ghqk,kgd->ghqd/dot_general | solution.py:134
  285.9 5.3 %fusion.10 = f32[4,256]{1,0:T(4,128)S(1)} fusion(f32[4,256,4096]{2,1,0:T(8,128)S(1)} %get-tuple-element.24, f32[4,256]{1,0:T(4,128)S(1)} %broadcast_maximum_fusion, pred[256,4096]{1,0:T(8,128)(4,1)S(1)} %get-tuple-element.20), kind=kLoop, calls=%fused_computation.19 | loop fusion | flops 20970496 | bytes 17833984 | tf_op jit(solution)/shard_map/reduce_sum | solution.py:133
  291.2 0.7 fusion.46
  292.0 0.8 copy.17
  292.8 0.0 copy-start.1
  292.8 15.3 %convolution_convert_fusion = bf16[1024,8192]{1,0:T(8,128)(2,1)} fusion(bf16[512,8192]{1,0:T(8,128)(2,1)} %param.10, bf16[128,8,4,128]{3,2,1,0:T(4,128)(2,1)S(1)} %bitcast.89), kind=kOutput, calls=%fused_computation.8 | convolution fusion | flops 8598323200 | bytes 26214400 | tf_op jit(solution)/shard_map/dot_general | solution.py:149
  308.1 0.0 reduce-scatter.2.cloned.1.call-update
  308.1 110.0 %reduce-scatter.2.cloned.1.call-done = bf16[64,8192]{1,0:T(8,128)(2,1)} async-done(((bf16[1024,8192]{1,0:T(8,128)(2,1)}), bf16[64,8192]{1,0:T(8,128)(2,1)}) %reduce-scatter.2.cloned.1.call-update) | async-done | bytes 1048592 | tf_op jit(solution)/shard_map/reduce_scatter | solution.py:148
  (26 shorter events, 0.1 us)
Async XLA Ops:
  6.5 118.5 %copy-start = (bf16[8192,128]{1,0:T(8,128)(2,1)S(1)}, bf16[8192,128]{1,0:T(8,128)(2,1)}, u32[]{:S(2)}) copy-start(bf16[8192,128]{1,0:T(8,128)(2,1)} %param.9) | copy-start | bytes 6291460
  6.5 118.5 %all-gather.3.cloned.1.call-start = ((), (), s32[]{:S(2)}) async-start(), calls=%async_computation.2 | async-start | bytes 17825792 | tf_op jit(solution)/shard_map/all_gather | solution.py:83
  10.8 178.8 %all-gather.5.cloned.1.call-start = ((), (), s32[]{:S(2)}) async-start(), calls=%async_computation.3 | async-start | bytes 4456448 | tf_op jit(solution)/shard_map/all_gather | solution.py:94
  192.3 33.7 %all-to-all-start = ((bf16[4,1024,256]{2,1,0:T(8,128)(2,1)}), bf16[4,1024,256]{2,1,0:T(8,128)(2,1)}, u32[]{:S(2)}, u32[]{:S(2)}) async-start(bf16[4,1024,256]{2,1,0:T(8,128)(2,1)} %broadcast_in_dim.65), calls=%async_computation | async-start | bytes 4194304 | tf_op jit(solution)/shard_map/all_to_all | solution.py:14
  197.5 220.6 %reduce-scatter.2.cloned.1.call-start = ((), (), s32[]{:S(2)}) async-start(), calls=%async_computation.4 | async-start | bytes 17825792 | tf_op jit(solution)/shard_map/reduce_scatter | solution.py:148
  224.3 6.7 %copy-start.4 = (pred[256,4096]{1,0:T(8,128)(4,1)S(1)}, pred[256,4096]{1,0:T(8,128)(4,1)}, u32[]{:S(2)}) copy-start(pred[256,4096]{1,0:T(8,128)(4,1)} %get-tuple-element.17) | copy-start | bytes 3145732
  226.0 10.3 %copy-start.5 = (pred[256,4096]{1,0:T(8,128)(4,1)S(1)}, pred[256,4096]{1,0:T(8,128)(4,1)}, u32[]{:S(2)}) copy-start(pred[256,4096]{1,0:T(8,128)(4,1)} %get-tuple-element.17) | copy-start | bytes 3145732
  236.3 6.3 %copy-start.3 = (pred[256,4096]{1,0:T(8,128)(4,1)S(1)}, pred[256,4096]{1,0:T(8,128)(4,1)}, u32[]{:S(2)}) copy-start(pred[256,4096]{1,0:T(8,128)(4,1)} %get-tuple-element.18) | copy-start | bytes 3145732
  236.3 6.3 %copy-start.6 = (bf16[4,256,1,4,128]{4,1,3,2,0:T(8,128)(2,1)S(1)}, bf16[4,256,1,4,128]{4,1,3,2,0:T(8,128)(2,1)}, u32[]{:S(2)}) copy-start(bf16[4,256,1,4,128]{4,1,3,2,0:T(8,128)(2,1)} %copy.26) | copy-start | bytes 3145732
  252.6 6.2 %copy-start.2 = (pred[256,4096]{1,0:T(8,128)(4,1)S(1)}, pred[256,4096]{1,0:T(8,128)(4,1)}, u32[]{:S(2)}) copy-start(pred[256,4096]{1,0:T(8,128)(4,1)} %get-tuple-element.19) | copy-start | bytes 3145732
  292.8 125.3 %copy-start.1 = (bf16[8192,128]{1,0:T(8,128)(2,1)S(1)}, bf16[8192,128]{1,0:T(8,128)(2,1)}, u32[]{:S(2)}) copy-start(bf16[8192,128]{1,0:T(8,128)(2,1)} %param.9) | copy-start | bytes 6291460
Sparse Core Ops, SparseCore 0:
  10.9 114.0 all-gather.2
  138.5 50.9 all-gather.4
  308.2 109.8 reduce-scatter.1
where the time goes:
time: 432 us; the launch traced here: 425 us
  waiting for transfers between devices  264 us (61%)
  matrix products  87.8 us (20%)
  other arithmetic  42.2 us (10%)
  between operations  14 us (3%)
  local copies, waits for them, and re-layouts  11.2 us (3%)
  starting transfers between devices  5.8 us (1%)
    all_gather x1, waiting for transfers between devices, local(): piece = lax.all_gather(normed, 'tp', axis=0, tiled=True)  113 us
    reduce_scatter x1, waiting for transfers between devices, local(): lax.psum_scatter(jnp.dot(heads_out, out_weight, preferred_element_type=jn...  110 us
    all_gather x1, waiting for transfers between devices, local(): kv_every = lax.all_gather(kv_part, 'tp', axis=1, tiled=True)  41.5 us
    dot_general x4, matrix products, local(): jnp.einsum('ghqk,kgd->ghqd', expd.astype(jnp.bfloat16), value_piece, pref...  24.7 us
    reduce_sum x4, other arithmetic, local(): total_new = jnp.sum(expd, axis=3)  21.1 us
    dot_general x4, matrix products, local(): jnp.einsum('ghqd,kgd->ghqk', q_here, key_piece, preferred_element_type=jn...  19.2 us
    dot_general x1, matrix products, local(): q_raw = jnp.dot(piece, q_weight, preferred_element_type=jnp.float32)  17.2 us
    dot_general x1, matrix products, local(): jnp.dot(heads_out, out_weight, preferred_element_type=jnp.float32)  15.3 us
  transfers between devices with their start and end apart: 4, of which 3 were waited for; matrix products, arithmetic and copies ran while one was open for 9% of the time, Pallas kernels for 0%

commit v1 on v0

--- a/solution.py
+++ b/solution.py
@@ -80,7 +80,9 @@
     ).astype(jnp.bfloat16)
     ends = jnp.cumsum(doc_lengths)
     is_key = tp_index * kv_cols < KVH * HD
-    piece = lax.all_gather(normed, "tp", axis=0, tiled=True)
+    piece = jnp.concatenate(
+        lax.all_to_all(jnp.stack([normed] * lax.axis_size("tp")), "tp", 0, 0), axis=0
+    )
     count = piece.shape[0]
     positions = ctx_index * ctx_rows + jnp.arange(count, dtype=jnp.int32)
     within = positions - doc_start(positions, doc_lengths, ends)

time: 432 us -> 580 us (1.34)
  waiting for transfers between devices: 264 us -> 395 us
  local copies, waits for them, and re-layouts: 11.2 us -> 28.8 us
  starting transfers between devices: 5.8 us -> 13.3 us
    all_to_all x0 -> x1, waiting for transfers between devices: none -> 249 us  [local(): lax.all_to_all(jnp.stack([normed] * lax.axis_size('tp')), 'tp', 0, 0)]
    all_gather x1 -> x0, waiting for transfers between devices: 113 us -> none  [local(): piece = lax.all_gather(normed, 'tp', axis=0, tiled=True)]
    dot_general x0 -> x1, local copies, waits for them, and re-layouts: none -> 11.3 us  [local(): q_raw = jnp.dot(piece, q_weight, preferred_element_type=jnp.float32)]
    all_gather x1, waiting for transfers between devices: 41.5 us -> 32.2 us  [local(): kv_every = lax.all_gather(kv_part, 'tp', axis=1, tiled=True)]
    all_to_all x0 -> x1, starting transfers between devices: none -> 7.76 us  [local(): lax.all_to_all(jnp.stack([normed] * lax.axis_size('tp')), 'tp', 0, 0)]
    another operation x0 -> x1, local copies, waits for them, and re-layouts: none -> 5.93 us  [local(): jnp.stack([normed] * lax.axis_size('tp'))]
  transfers between devices with their start and end apart: 4 -> 4, of which waited for: 3 -> 4; matrix products, arithmetic and copies ran while one was open for 9% -> 7% of each run, Pallas kernels for 0% -> 0%
where the time goes in v1:
time: 580 us; the launch traced here: 573 us
  waiting for transfers between devices  395 us (68%)
  matrix products  85.1 us (15%)
  other arithmetic  36.8 us (6%)
  local copies, waits for them, and re-layouts  28.8 us (5%)
  between operations  13.9 us (2%)
  starting transfers between devices  13.3 us (2%)
    all_to_all x1, waiting for transfers between devices, local(): lax.all_to_all(jnp.stack([normed] * lax.axis_size('tp')), 'tp', 0, 0)  249 us
    reduce_scatter x1, waiting for transfers between devices, local(): lax.psum_scatter(jnp.dot(heads_out, out_weight, preferred_element_type=jn...  111 us
    all_gather x1, waiting for transfers between devices, local(): kv_every = lax.all_gather(kv_part, 'tp', axis=1, tiled=True)  32.2 us
    dot_general x4, matrix products, local(): jnp.einsum('ghqk,kgd->ghqd', expd.astype(jnp.bfloat16), value_piece, pref...  24.6 us
    reduce_sum x4, other arithmetic, local(): total_new = jnp.sum(expd, axis=3)  20.8 us
    dot_general x4, matrix products, local(): jnp.einsum('ghqd,kgd->ghqk', q_here, key_piece, preferred_element_type=jn...  19.4 us
    dot_general x1, matrix products, local(): jnp.dot(heads_out, out_weight, preferred_element_type=jnp.float32)  15.3 us
    dot_general x1, matrix products, local(): q_raw = jnp.dot(piece, q_weight, preferred_element_type=jnp.float32)  14.4 us
  transfers between devices with their start and end apart: 4, of which 4 were waited for; matrix products, arithmetic and copies ran while one was open for 7% of the time, Pallas kernels for 0%

profile of v1, /device:TPU:1, one launch (start us, length us, event | category | flops | bytes accessed | tf_op | source)
XLA Modules:
  0.0 573.0 jit_solution(3448706338425159235)
XLA Ops:
  6.5 1.7 fusion.28
  8.2 1.5 fusion.30
  9.8 5.9 %stack.22 = bf16[16,64,8192]{2,1,0:T(8,128)(2,1)} broadcast(bf16[64,8192]{1,0:T(8,128)(2,1)S(1)} %fusion.30), dimensions={1,2} | broadcast | bytes 17825792 | tf_op jit(solution)/shard_map/stack | solution.py:84
  15.7 7.8 %all-to-all-start = ((bf16[16,64,8192]{2,1,0:T(8,128)(2,1)}), bf16[16,64,8192]{2,1,0:T(8,128)(2,1)}, u32[]{:S(2)}, u32[]{:S(2)}) async-start(bf16[16,64,8192]{2,1,0:T(8,128)(2,1)} %stack.22), calls=%async_computation | async-start | bytes 33554432 | tf_op jit(solution)/shard_map/all_to_all | solution.py:84
  23.5 0.0 all-gather.2.cloned.1.call-start
  23.5 0.2 reduce-window.8
  23.8 0.1 select_reduce_fusion
  23.9 248.7 %all-to-all-done = bf16[16,64,8192]{2,1,0:T(8,128)(2,1)} async-done(((bf16[16,64,8192]{2,1,0:T(8,128)(2,1)}), bf16[16,64,8192]{2,1,0:T(8,128)(2,1)}, u32[]{:S(2)}, u32[]{:S(2)}) %all-to-all-start) | async-done | bytes 16777248 | tf_op jit(solution)/shard_map/all_to_all | solution.py:84
  272.6 11.4 %fusion.72 = f32[1024,128]{0,1:T(8,128)S(1)} fusion(bf16[1024,8192]{1,0:T(8,128)(2,1)} %bitcast.2, bf16[8192,128]{1,0:T(8,128)(2,1)S(1)} %copy-done), kind=kOutput, calls=%fused_computation.114 | convolution fusion | flops 2147483648 | bytes 19398656 | tf_op jit(solution)/shard_map/dot_general | solution.py:90
  284.0 1.2 fusion.57
  285.2 0.8 fusion.48
  286.0 0.0 all-gather.2.cloned.1.call-update
  286.0 11.3 %copy.18 = bf16[512,8192]{1,0:T(8,128)(2,1)} copy(bf16[512,8192]{0,1:T(8,128)(2,1)} %bitcast.85) | data formatting | bytes 16777216 | tf_op jit(solution)/shard_map/dot_general | solution.py:89
  297.3 0.1 convert_reduce_fusion.4
  297.4 0.1 convert_reduce_fusion
  297.5 1.7 multiply_cosine_fusion.1
  299.3 5.6 fusion.24
  304.8 32.2 %all-gather.2.cloned.1.call-done = bf16[1024,2048]{0,1:T(8,128)(2,1)} async-done(((bf16[1024,128]{0,1:T(8,128)(2,1)}), bf16[1024,2048]{0,1:T(8,128)(2,1)}) %all-gather.2.cloned.1.call-update) | async-done | bytes 4194320 | tf_op jit(solution)/shard_map/all_gather | solution.py:96
  337.0 1.1 constant_dynamic-slice_fusion.1
  338.1 0.9 pad_maximum_fusion.1
  339.0 2.1 copy.16
  341.1 2.5 broadcast_in_dim.65
  343.6 5.3 all-to-all-start.1
  348.9 0.2 reduce-scatter.2.cloned.1.call-start
  349.1 14.4 %fusion.71 = f32[1024,4,128]{0,2,1:T(8,128)S(1)} fusion(bf16[1024,8192,1]{1,0,2:T(8,128)(2,1)} %bitcast.3, bf16[4,128,8192]{2,1,0:T(8,128)(2,1)} %bitcast.86), kind=kOutput, calls=%fused_computation.113 | convolution fusion | flops 8589934592 | bytes 27262976 | tf_op jit(solution)/shard_map/dot_general | solution.py:89
  363.5 0.4 subtract_convert_fusion
  363.9 1.1 pad_maximum_fusion
  365.0 2.7 convert_element_type.78
  367.6 2.5 copy.15
  370.1 3.6 all-to-all-done.1
  373.7 5.0 fusion.1
  378.7 5.0 fusion.6
  383.8 6.2 %fusion.35 = f32[1,1,4,256,128]{4,3,2,1,0:T(8,128)S(1)} fusion(f32[4,256,4096]{2,1,0:T(8,128)S(1)} %get-tuple-element.26, f32[4,256]{1,0:T(4,128)S(1)} %broadcast_maximum_fusion.2, pred[256,4096]{1,0:T(8,128)(4,1)S(1)} %copy-done.2, bf16[4096,256]{1,0:T(8,128)(2,1)} %bitcast.10), kind=kOutput, calls=%fused_computation.45 | convolution fusion | flops 1094713344 | bytes 19402752 | tf_op jit(solution)/shard_map/ghqk,kgd->ghqd/dot_general | solution.py:136
  390.0 4.9 fusion.2
  395.0 5.1 fusion.8
  400.0 6.1 %fusion.38 = f32[1,1,4,256,128]{4,3,2,1,0:T(8,128)S(1)} fusion(f32[4,256,4096]{2,1,0:T(8,128)S(1)} %get-tuple-element.24, f32[4,256]{1,0:T(4,128)S(1)} %broadcast_maximum_fusion.1, pred[256,4096]{1,0:T(8,128)(4,1)S(1)} %get-tuple-element.17, bf16[4096,256]{1,0:T(8,128)(2,1)} %bitcast.10), kind=kOutput, calls=%fused_computation.46 | convolution fusion | flops 1094713344 | bytes 19402752 | tf_op jit(solution)/shard_map/ghqk,kgd->ghqd/dot_general | solution.py:136
  406.1 4.7 fusion.3
  410.9 5.4 fusion.10
  416.3 6.1 %fusion.41 = f32[1,1,4,256,128]{4,3,2,1,0:T(8,128)S(1)} fusion(f32[4,256,4096]{2,1,0:T(8,128)S(1)} %get-tuple-element.22, f32[4,256]{1,0:T(4,128)S(1)} %broadcast_maximum_fusion, pred[256,4096]{1,0:T(8,128)(4,1)S(1)} %get-tuple-element.18, bf16[4096,256]{1,0:T(8,128)(2,1)} %bitcast.10), kind=kOutput, calls=%fused_computation.47 | convolution fusion | flops 1094713344 | bytes 19402752 | tf_op jit(solution)/shard_map/ghqk,kgd->ghqd/dot_general | solution.py:136
  422.5 4.7 fusion
  427.2 6.1 %fusion.32 = f32[1,1,4,256,128]{4,3,2,1,0:T(8,128)S(1)} fusion(f32[4,256,4096]{2,1,0:T(8,128)S(1)} %get-tuple-element.28, f32[4,256]{1,0:T(4,128)S(1)} %broadcast_maximum_fusion.3, pred[256,4096]{1,0:T(8,128)(4,1)S(1)} %get-tuple-element.15, bf16[4096,256]{1,0:T(8,128)(2,1)} %bitcast.10), kind=kOutput, calls=%fused_computation.44 | convolution fusion | flops 1094713344 | bytes 19402752 | tf_op jit(solution)/shard_map/ghqk,kgd->ghqd/dot_general | solution.py:136
  433.3 5.2 fusion.4
  438.6 0.7 fusion.46
  439.3 0.8 copy.17
  440.1 0.0 copy-start.1
  440.2 15.3 %convolution_convert_fusion = bf16[1024,8192]{1,0:T(8,128)(2,1)} fusion(bf16[512,8192]{1,0:T(8,128)(2,1)} %param.10, bf16[128,8,4,128]{3,2,1,0:T(4,128)(2,1)S(1)} %bitcast.92), kind=kOutput, calls=%fused_computation.8 | convolution fusion | flops 8598323200 | bytes 26214400 | tf_op jit(solution)/shard_map/dot_general | solution.py:151
  455.4 0.0 reduce-scatter.2.cloned.1.call-update
  455.4 110.5 %reduce-scatter.2.cloned.1.call-done = bf16[64,8192]{1,0:T(8,128)(2,1)} async-done(((bf16[1024,8192]{1,0:T(8,128)(2,1)}), bf16[64,8192]{1,0:T(8,128)(2,1)}) %reduce-scatter.2.cloned.1.call-update) | async-done | bytes 1048592 | tf_op jit(solution)/shard_map/reduce_scatter | solution.py:150
  (23 shorter events, 0.1 us)
Async XLA Ops:
  6.5 266.1 %copy-start = (bf16[8192,128]{1,0:T(8,128)(2,1)S(1)}, bf16[8192,128]{1,0:T(8,128)(2,1)}, u32[]{:S(2)}) copy-start(bf16[8192,128]{1,0:T(8,128)(2,1)} %param.9) | copy-start | bytes 6291460
  15.7 7.8 %copy-start.5 = (s32[8]{0:T(128)S(1)}, s32[8]{0:T(128)}, u32[]{:S(2)}) copy-start(s32[8]{0:T(128)} %param.11) | copy-start | bytes 100
  15.7 256.9 %all-to-all-start = ((bf16[16,64,8192]{2,1,0:T(8,128)(2,1)}), bf16[16,64,8192]{2,1,0:T(8,128)(2,1)}, u32[]{:S(2)}, u32[]{:S(2)}) async-start(bf16[16,64,8192]{2,1,0:T(8,128)(2,1)} %stack.22), calls=%async_computation | async-start | bytes 33554432 | tf_op jit(solution)/shard_map/all_to_all | solution.py:84
  23.5 313.6 %all-gather.2.cloned.1.call-start = ((), (), s32[]{:S(2)}) async-start(), calls=%async_computation.3 | async-start | bytes 4456448 | tf_op jit(solution)/shard_map/all_gather | solution.py:96
  343.6 30.1 %all-to-all-start.1 = ((bf16[4,1024,256]{2,1,0:T(8,128)(2,1)}), bf16[4,1024,256]{2,1,0:T(8,128)(2,1)}, u32[]{:S(2)}, u32[]{:S(2)}) async-start(bf16[4,1024,256]{2,1,0:T(8,128)(2,1)} %broadcast_in_dim.65), calls=%async_computation.1 | async-start | bytes 4194304 | tf_op jit(solution)/shard_map/all_to_all | solution.py:14
  348.9 217.1 %reduce-scatter.2.cloned.1.call-start = ((), (), s32[]{:S(2)}) async-start(), calls=%async_computation.4 | async-start | bytes 17825792 | tf_op jit(solution)/shard_map/reduce_scatter | solution.py:150
  349.1 14.4 %copy-start.3 = (f32[1024,64]{0,1:T(8,128)S(1)}, f32[1024,64]{0,1:T(8,128)}, u32[]{:S(2)}) copy-start(f32[1024,64]{0,1:T(8,128)} %get-tuple-element.20) | copy-start | bytes 786436
  373.7 5.0 copy-start.2
  383.8 6.2 %copy-start.4 = (bf16[4,256,1,4,128]{4,1,3,2,0:T(8,128)(2,1)S(1)}, bf16[4,256,1,4,128]{4,1,3,2,0:T(8,128)(2,1)}, u32[]{:S(2)}) copy-start(bf16[4,256,1,4,128]{4,1,3,2,0:T(8,128)(2,1)} %copy.15) | copy-start | bytes 3145732
  440.1 125.8 %copy-start.1 = (bf16[8192,128]{1,0:T(8,128)(2,1)S(1)}, bf16[8192,128]{1,0:T(8,128)(2,1)}, u32[]{:S(2)}) copy-start(bf16[8192,128]{1,0:T(8,128)(2,1)} %param.9) | copy-start | bytes 6291460
Sparse Core Ops, SparseCore 0:
  286.1 50.8 all-gather.1
  455.6 110.3 reduce-scatter.1
